TPU v7x, 128 devices: a whole 4x4x4 slice. The times are simulated.
128 devices in a mesh: seq: 16 (over z, x), req: 8 (over y, core).
Axes of the slice: x: 4, y: 4, z: 4, core: 2. Of those that a mesh axis runs over, the one named last changes fastest.
Arguments:
- given_token_index: int32 [128], replicated, may hold values from 0 to 31999
- hidden: bfloat16 [128, 3584], P('req'), may hold values from -6 to 6
- token_embedding_table: bfloat16 [32000, 3584], P(('seq', 'req')), may hold values from -6 to 6
- attention_norm_gain: bfloat16 [7168], replicated, may hold values from 0.099609375 to 1.8984375
- query_key_value_weight: bfloat16 [7168, 10752], P('req', 'seq'), may hold values from -0.0625 to 0.0625
- rotated_key_cache: bfloat16 [96, 8, 128, 3584], P('seq', 'req'), may hold values from -240 to 240
- cached_value_pages: bfloat16 [96, 8, 128, 3584], P('seq', 'req'), may hold values from -6 to 6
- lengths: int32 [32], P('req'), may hold values from 1 to 6144, as said below
- request_page_slots: int32 [32, 48], P('req'), may hold values from 0 to 95, as said below
- attention_output_weight: bfloat16 [3584, 7168], P('seq'), may hold values from -0.375 to 0.375
- feedforward_norm_gain: bfloat16 [7168], replicated, may hold values from 0.099609375 to 1.8984375
- gate_weight: bfloat16 [7168, 14336], P('req', 'seq'), may hold values from -0.0625 to 0.0625
- up_weight: bfloat16 [7168, 14336], P('req', 'seq'), may hold values from -0.0625 to 0.0625
- adapter_down_map: bfloat16 [7168, 128], P('req'), may hold values from -0.0625 to 0.0625
- adapter_gate_map: bfloat16 [128, 14336], P(None, 'seq'), may hold values from -0.5 to 0.5
- adapter_up_map: bfloat16 [128, 14336], P(None, 'seq'), may hold values from -0.5 to 0.5
- down_weight: bfloat16 [14336, 7168], P('seq', 'req'), may hold values from -0.046875 to 0.046875
Outputs:
- block_out: bfloat16 [128, 7168], P('seq', 'req')
Inputs may be any that keep to these rules, and one draw needn't show every extreme that they name: `lengths`: in each group of 4 requests exactly one has 6144 tokens, and the pages of a group's requests number at most 96 together. `request_page_slots`: entry p of request i names a slot of its group, 0 to 95; the entries with p * 128 below lengths[i] are distinct within a group, the others name any slot. Slot g of a group lies on the seq index g // 6, at place g % 6.
All inputs are finite; a program needn't handle non-finite values.
Results may differ from a plain program's by a relative error of at most 0.028.
The roundings to bfloat16 on the way count: a program that leaves them out, or rounds other values in their place, can miss the bound.
Values may be sent and summed in bfloat16 or wider, within the bound.
A program may use at most 128 MiB of HBM per device.

v0:
```python
import math
import jax
import jax.numpy as jnp
from jax import lax
from jax.sharding import PartitionSpec as P

HEADS = 16
HD = 224
NEGATIVE = -1e30
EPSILON = 1e-05
ROTARY_BASE = 10000.0


def merged_2(array, axis, combine):
    everything = jax.tree.map(lambda part: lax.all_gather(part, axis), array)
    first = jax.tree.map(lambda part: part[0], everything)

    def hop(k, so_far):
        return combine(so_far, jax.tree.map(lambda part: part[k], everything))

    return lax.fori_loop(1, lax.axis_size(axis), hop, first)


def rms_norm(matrix, gain_vec):
    widened = matrix.astype(jnp.float32)
    factor = lax.rsqrt(jnp.mean(widened * widened, axis=-1, keepdims=True) + EPSILON)
    return (widened * factor * gain_vec.astype(jnp.float32)).astype(jnp.bfloat16)


def rotate(vectors, positions):
    half_dim = vectors.shape[-1] // 2
    frequency = ROTARY_BASE ** (-2.0 * jnp.arange(half_dim, dtype=jnp.float32) / vectors.shape[-1])
    angles = positions.astype(jnp.float32)[..., None, None] * frequency
    cosine = jnp.cos(angles)
    sine_part = jnp.sin(angles)
    front_half = vectors[..., :half_dim]
    back_half = vectors[..., half_dim:]
    return jnp.concatenate(
        [front_half * cosine - back_half * sine_part, back_half * cosine + front_half * sine_part],
        axis=-1,
    )


def softmax_join(earlier, later):
    first_max, first_sum, first_out = earlier
    second_max, second_sum, second_out = later
    overall = jnp.maximum(first_max, second_max)
    first_factor = jnp.exp(first_max - overall)
    second_factor = jnp.exp(second_max - overall)
    return (
        overall,
        first_sum * first_factor + second_sum * second_factor,
        first_out * first_factor[..., None] + second_out * second_factor[..., None],
    )


def body(
    given_token_index,
    hidden,
    token_embedding_table,
    attention_norm_gain,
    query_key_value_weight,
    rotated_key_cache,
    cached_value_pages,
    lengths,
    request_page_slots,
    attention_output_weight,
    feedforward_norm_gain,
    gate_weight,
    up_weight,
    adapter_down_map,
    adapter_gate_map,
    adapter_up_map,
    down_weight,
):
    seq_devices = lax.axis_size("seq")
    req_devices = lax.axis_size("req")
    seq_index = lax.axis_index("seq")
    req_index = lax.axis_index("req")
    group_rows = hidden.shape[0]
    requests = lengths.shape[0]
    steps_each = group_rows // requests
    vocab_rows = token_embedding_table.shape[0]
    first_id = (seq_index * req_devices + req_index) * vocab_rows
    local_ids = given_token_index - first_id
    present = (local_ids >= 0) & (local_ids < vocab_rows)
    looked = jnp.take(token_embedding_table, jnp.clip(local_ids, 0, vocab_rows - 1), axis=0).astype(
        jnp.float32
    )
    looked = jnp.where(present[:, None], looked, 0.0)
    everywhere = lax.psum(looked, ("seq", "req"))
    embedded = lax.dynamic_slice_in_dim(everywhere, req_index * group_rows, group_rows, 0)
    joined = jnp.concatenate([hidden, embedded.astype(jnp.bfloat16)], axis=1)
    normed = rms_norm(joined, attention_norm_gain)
    spread = lax.all_to_all(normed, "req", split_axis=1, concat_axis=0, tiled=True)
    block_rows = spread
    qkv_part = lax.psum_scatter(
        jnp.dot(block_rows, query_key_value_weight, preferred_element_type=jnp.float32),
        "req",
        scatter_dimension=0,
        tiled=True,
    )
    projected = lax.all_gather(qkv_part.astype(jnp.bfloat16), "seq", axis=1, tiled=True)
    head_cols = HEADS * HD
    queries = projected[:, :head_cols].reshape(requests, steps_each, HEADS, HD)
    new_keys = projected[:, head_cols : 2 * head_cols].reshape(requests, steps_each, HEADS, HD)
    new_values = projected[:, 2 * head_cols :].reshape(requests, steps_each, HEADS, HD)
    positions = lengths[:, None] + jnp.arange(steps_each, dtype=jnp.int32)[None, :]
    queries = rotate(queries.astype(jnp.float32), positions).astype(jnp.bfloat16)
    new_keys = rotate(new_keys.astype(jnp.float32), positions).astype(jnp.bfloat16)
    slots = rotated_key_cache.shape[0]
    page_len = rotated_key_cache.shape[2]
    cache_k = rotated_key_cache.reshape(slots * page_len, HEADS, HD)
    cache_v = cached_value_pages.reshape(slots * page_len, HEADS, HD)
    slot_ids = seq_index * slots + jnp.arange(slots, dtype=jnp.int32)
    page_ids = jnp.arange(request_page_slots.shape[1], dtype=jnp.int32)
    is_live = page_ids[None, :] < ((lengths + page_len - 1) // page_len)[:, None]
    matches = (request_page_slots[:, :, None] == slot_ids[None, None, :]) & is_live[:, :, None]
    is_owned = jnp.any(matches, axis=1)
    page_of = jnp.sum(jnp.where(matches, page_ids[None, :, None], 0), axis=1)
    token_pos = (
        page_of[:, :, None] * page_len + jnp.arange(page_len, dtype=jnp.int32)[None, None, :]
    )
    is_valid = (is_owned[:, :, None] & (token_pos < lengths[:, None, None])).reshape(
        requests, slots * page_len
    )
    score_scale = 1.0 / math.sqrt(HD)
    scores = (
        jnp.einsum("rthd,khd->rthk", queries, cache_k, preferred_element_type=jnp.float32)
        * score_scale
    )
    mask_b = is_valid[:, None, None, :]
    local_max = jnp.max(jnp.where(mask_b, scores, NEGATIVE), axis=-1)
    weights = jnp.where(mask_b, jnp.exp(scores - local_max[..., None]), 0.0)
    local_sum = jnp.sum(weights, axis=-1)
    local_out = jnp.einsum(
        "rthk,khd->rthd", weights.astype(jnp.bfloat16), cache_v, preferred_element_type=jnp.float32
    )
    fresh_scores = (
        jnp.einsum("rthd,rshd->rths", queries, new_keys, preferred_element_type=jnp.float32)
        * score_scale
    )
    causal = jnp.arange(steps_each)[:, None] >= jnp.arange(steps_each)[None, :]
    fresh_mask = causal[None, :, None, :]
    fresh_max = jnp.max(jnp.where(fresh_mask, fresh_scores, NEGATIVE), axis=-1)
    fresh_w = jnp.where(fresh_mask, jnp.exp(fresh_scores - fresh_max[..., None]), 0.0)
    fresh_sum = jnp.sum(fresh_w, axis=-1)
    fresh_out = jnp.einsum(
        "rths,rshd->rthd",
        fresh_w.astype(jnp.bfloat16),
        new_values,
        preferred_element_type=jnp.float32,
    )
    own_heads = HEADS // seq_devices
    first_head = seq_index * own_heads

    def own_slice(member):
        return lax.dynamic_slice_in_dim(member, first_head, own_heads, 2)

    fresh_part = (own_slice(fresh_max), own_slice(fresh_sum), own_slice(fresh_out))
    merged = merged_2((local_max, local_sum, local_out), "seq", softmax_join)
    combined = softmax_join(tuple((own_slice(member) for member in merged)), fresh_part)
    attention = (
        (combined[2] / combined[1][..., None])
        .astype(jnp.bfloat16)
        .reshape(group_rows, own_heads * HD)
    )
    projected_out = jnp.dot(attention, attention_output_weight, preferred_element_type=jnp.float32)
    mixed_sum = lax.psum(projected_out, "seq")
    after_attn = (joined.astype(jnp.float32) + mixed_sum).astype(jnp.bfloat16)
    second_normed_state = rms_norm(after_attn, feedforward_norm_gain)
    residual_cols, second_spread_state = (
        lax.all_to_all(after_attn, "req", split_axis=1, concat_axis=0, tiled=True),
        lax.all_to_all(second_normed_state, "req", split_axis=1, concat_axis=0, tiled=True),
    )
    gate_total, up_total, low_sum = lax.psum(
        (
            jnp.dot(second_spread_state, gate_weight, preferred_element_type=jnp.float32),
            jnp.dot(second_spread_state, up_weight, preferred_element_type=jnp.float32),
            jnp.dot(second_spread_state, adapter_down_map, preferred_element_type=jnp.float32),
        ),
        "req",
    )
    adapter_hidden = low_sum.astype(jnp.bfloat16)
    gate_preactivation = gate_total + jnp.dot(
        adapter_hidden, adapter_gate_map, preferred_element_type=jnp.float32
    )
    up_projection_part = up_total + jnp.dot(
        adapter_hidden, adapter_up_map, preferred_element_type=jnp.float32
    )
    inner_act = (jax.nn.silu(gate_preactivation) * up_projection_part).astype(jnp.bfloat16)
    out_rows = residual_cols.shape[0] // seq_devices
    block_rows = inner_act
    down_sum = lax.psum_scatter(
        jnp.dot(block_rows, down_weight, preferred_element_type=jnp.float32),
        "seq",
        scatter_dimension=0,
        tiled=True,
    )
    residual_rows = lax.dynamic_slice_in_dim(residual_cols, seq_index * out_rows, out_rows, 0)
    return (residual_rows.astype(jnp.float32) + down_sum).astype(jnp.bfloat16)


def solution(mesh):
    placed = (
        P(),
        P("req", None),
        P(("seq", "req"), None),
        P(),
        P("req", "seq"),
        P("seq", "req", None, None),
        P("seq", "req", None, None),
        P("req"),
        P("req", None),
        P("seq", None),
        P(),
        P("req", "seq"),
        P("req", "seq"),
        P("req", None),
        P(None, "seq"),
        P(None, "seq"),
        P("seq", "req"),
    )
    return jax.shard_map(
        body, mesh=mesh, in_specs=placed, out_specs=P("seq", "req"), check_vma=False
    )
```

profile of v0, /device:TPU:0, one launch (start us, length us, event | category | flops | bytes accessed | tf_op | source)
XLA Modules:
  0.0 529.0 jit_solution(585776612457046075)
XLA Ops:
  7.4 4.9 gather_fusion
  12.2 2.8 convert_select_fusion
  15.0 74.1 %all-reduce.12 = bf16[128,3584]{1,0:T(8,128)(2,1)} all-reduce(f32[128,3584]{1,0:T(8,128)} %convert_select_fusion), channel_id=1, replica_groups=mesh['seq'=16,'req'=8] {'seq','req'}, use_global_device_ids=true, to_apply=%region_0.1 | all-reduce | flops 458752 | bytes 2752512 | tf_op jit(solution)/shard_map/psum | solution.py:91
  94.6 3.9 all-to-all-start
  106.7 2.6 fusion.67
  110.2 13.1 %reshape.185 = bf16[768,16,224]{2,1,0:T(8,128)(2,1)} reshape(bf16[6,1,128,3584]{3,2,1,0:T(8,128)(2,1)} %param.24) | data formatting | bytes 11010048 | tf_op jit(solution)/shard_map/reshape | solution.py:113
  123.3 13.2 %reshape.186 = bf16[768,16,224]{2,1,0:T(8,128)(2,1)} reshape(bf16[6,1,128,3584]{3,2,1,0:T(8,128)(2,1)} %param.25) | data formatting | bytes 11010048 | tf_op jit(solution)/shard_map/reshape | solution.py:114
  139.9 24.2 %all-gather.3 = bf16[16,672,16]{1,2,0:T(8,128)(2,1)S(1)} all-gather(bf16[1,672,16]{1,2,0:T(8,128)(2,1)S(1)} %convert_bitcast_fusion), channel_id=1, replica_groups=mesh['seq'=16,'req'=8] {'seq'}, dimensions={0}, use_global_device_ids=true | all-gather | bytes 365568 | tf_op jit(solution)/shard_map/all_gather | solution.py:103
  165.0 1.5 reshape.211
  171.9 6.8 %select_reduce_fusion = (f32[4,4,16]{1,0,2:T(4,128)S(1)}, f32[4,4,16,768]{3,1,0,2:T(4,128)S(1)}) fusion(pred[4,768]{1,0:T(4,128)(4,1)} %fusion.54, bf16[768,16,224,1]{2,1,0,3:T(8,128)(2,1)} %bitcast.116, bf16[4,4,16,112]{3,1,0,2:T(4,128)(2,1)S(1)} %get-tuple-element.268, bf16[4,4,16,112]{3,1,0,2:T(4,128)(2,1)S(1)} %get-tuple-element.269), kind=kOutput, calls=%fused_computation.25 | convolution fusion | flops 88899328 | bytes 6410240 | tf_op jit(solution)/shard_map/rthd,khd->rthk/dot_general | solution.py:129
  179.7 4.6 fusion.16
  185.6 2.3 fusion.21
  188.7 22.9 %all-gather.1 = f32[64,4,16]{2,1,0:T(4,128)S(1)} all-gather(f32[4,4,16]{2,1,0:T(4,128)S(1)} %copy.119), channel_id=3, replica_groups=mesh['seq'=16,'req'=8] {'seq'}, dimensions={0}, use_global_device_ids=true | all-gather | bytes 17408 | tf_op jit(solution)/shard_map/all_gather | solution.py:15
  211.7 21.9 %all-gather = f32[64,4,16]{2,1,0:T(4,128)S(1)} all-gather(f32[4,4,16]{2,1,0:T(4,128)} %copy.118), channel_id=2, replica_groups=mesh['seq'=16,'req'=8] {'seq'}, dimensions={0}, use_global_device_ids=true | all-gather | bytes 17408 | tf_op jit(solution)/shard_map/all_gather | solution.py:15
  242.3 29.8 %while.19 = (s32[]{:T(128)}, f32[4,4,16]{2,1,0:T(4,128)S(1)}, f32[4,4,16]{2,1,0:T(4,128)S(1)}, f32[4,4,16,224]{3,2,1,0:T(8,128)S(1)}, f32[16,4,4,16]{3,2,1,0:T(4...) while((s32[]{:T(128)}, f32[4,4,16]{2,1,0:T(4,128)S(1)}, ...), condition=%wide.region_8.9_spmd, body=%wide.region_7.8_spmd.sunk | while | flops 173573 | bytes 1157271 | solution.py:21
  275.5 81.3 %all-reduce.7.cloned.1.call-done = f32[16,7168]{1,0:T(8,128)} async-done(((f32[16,7168]{1,0:T(8,128)}), f32[16,7168]{1,0:T(8,128)}) %all-reduce.7.cloned.1.call-update) | async-done | bytes 458768 | tf_op jit(solution)/shard_map/psum | solution.py:169
  358.2 11.4 %all_to_all.54 = bf16[16,8,896]{2,0,1:T(8,128)(2,1)S(1)} all-to-all(bf16[16,8,896]{2,0,1:T(8,128)(2,1)S(1)} %bitcast.125), channel_id=1, replica_groups=mesh['seq'=16,'req'=8] {'req'}, dimensions={1} | all-to-all | bytes 458752 | tf_op jit(solution)/shard_map/all_to_all | solution.py:174
  373.4 24.2 %psum.38 = bf16[128,128]{1,0:T(8,128)(2,1)S(1)} all-reduce(f32[128,128]{1,0:T(8,128)S(1)} %fusion.70), channel_id=1, replica_groups=mesh['seq'=16,'req'=8] {'req'}, use_global_device_ids=true, to_apply=%region_14.15 | all-reduce | flops 16384 | bytes 98304 | tf_op jit(solution)/shard_map/psum | solution.py:176
  397.5 34.2 %all-reduce.11.cloned.1.call-done = (f32[128,896]{1,0:T(8,128)}, f32[128,896]{1,0:T(8,128)}) async-done(((f32[128,896]{1,0:T(8,128)}, f32[128,896]{1,0:T(8,128)}), (f32[128,896]{1,0:T(8,128)}, f32[128,896]{1,0:T(8,128)})) %all-reduce.11.cloned.1.call-update) | async-done | bytes 917520 | tf_op jit(solution)/shard_map/psum | solution.py:176
  431.8 2.1 convolution_add_fusion.1
  433.9 3.2 fusion.19
  437.9 3.4 all-to-all-start.1
  442.5 5.9 %all-to-all-done.1 = bf16[16,8,896]{2,0,1:T(8,128)(2,1)S(1)} async-done(((bf16[16,8,896]{2,0,1:T(8,128)(2,1)}), bf16[16,8,896]{2,0,1:T(8,128)(2,1)S(1)}, u32[]{:S(2)}, u32[]{:S(2)}) %all-to-all-start.1) | async-done | bytes 229408 | tf_op jit(solution)/shard_map/all_to_all | solution.py:173
  448.4 72.7 %all-reduce.9.cloned.1.call-done = f32[128,896]{1,0:T(8,128)} async-done(((f32[128,896]{1,0:T(8,128)}), f32[128,896]{1,0:T(8,128)}) %all-reduce.9.cloned.1.call-update) | async-done | bytes 458768
  (179 shorter events, 77.3 us)
Async XLA Ops:
  6.5 267.5 %copy-start = (bf16[224,7168]{1,0:T(8,128)(2,1)S(1)}, bf16[224,7168]{1,0:T(8,128)(2,1)}, u32[]{:S(2)}) copy-start(bf16[224,7168]{1,0:T(8,128)(2,1)} %param.28) | copy-start | bytes 9633796
  15.0 75.1 %copy-start.7 = (bf16[16,3584]{1,0:T(8,128)(2,1)S(1)}, bf16[16,3584]{1,0:T(8,128)(2,1)}, u32[]{:S(2)}) copy-start(bf16[16,3584]{1,0:T(8,128)(2,1)} %param.20) | copy-start | bytes 344068
  90.0 19.3 %copy-start.3 = (bf16[16,3584]{1,0:T(8,128)(2,1)}, bf16[16,3584]{1,0:T(8,128)(2,1)S(1)}, u32[]{:S(2)}) copy-start(bf16[16,3584]{1,0:T(8,128)(2,1)S(1)} %dynamic-slice_convert_fusion) | copy-start | bytes 344068
  94.6 12.1 %all-to-all-start = ((bf16[16,8,896]{2,0,1:T(8,128)(2,1)}), bf16[16,8,896]{2,0,1:T(8,128)(2,1)S(1)}, u32[]{:S(2)}, u32[]{:S(2)}) async-start(bf16[16,8,896]{2,0,1:T(8,128)(2,1)} %copy.113), calls=%async_computation | async-start | bytes 458752 | tf_op jit(solution)/shard_map/all_to_all | solution.py:95
  98.5 40.6 %reduce-scatter.2.cloned.1.call-start = ((), (), s32[]{:S(2)}) async-start(), calls=%async_computation.4 | async-start | bytes 442368 | tf_op jit(solution)/shard_map/reduce_scatter | solution.py:97
  109.3 131.8 %all-gather.6.cloned.1.call-start = ((), (), s32[]{:S(2)}) async-start(), calls=%async_computation.6 | async-start | bytes 4456448 | tf_op jit(solution)/shard_map/all_gather | solution.py:15
  123.3 13.2 %copy-start.20 = (f32[4,4]{1,0:T(4,128)S(1)}, f32[4,4]{1,0:T(4,128)}, u32[]{:S(2)}) copy-start(f32[4,4]{1,0:T(4,128)} %add_convert_fusion.2) | copy-start | bytes 196
  123.3 14.0 %copy-start.16 = (s32[768]{0:T(1024)S(1)}, s32[768]{0:T(1024)}, u32[]{:S(2)}) copy-start(s32[768]{0:T(1024)} %iota_bitcast_fusion) | copy-start | bytes 9220
  123.3 14.0 %copy-start.17 = (pred[1,4,6,128]{3,2,1,0:T(8,128)(4,1)S(1)}, pred[1,4,6,128]{3,2,1,0:T(8,128)(4,1)}, u32[]{:S(2)}) copy-start(pred[1,4,6,128]{3,2,1,0:T(8,128)(4,1)} %broadcast_bitcast_fusion.1) | copy-start | bytes 9220
  123.3 14.0 %copy-start.21 = (s32[4]{0:T(128)S(1)}, s32[4]{0:T(128)}, u32[]{:S(2)}) copy-start(s32[4]{0:T(128)} %param.26) | copy-start | bytes 52
  170.5 9.2 %slice-start = ((s8[6291456]{0:T(1024)(128)(4,1)}), s8[4194304]{0:T(1024)(128)(4,1)S(1)}, s32[]{:S(2)}) async-start(s8[6291456]{0:T(1024)(128)(4,1)} %bitcast.113), calls=%async_computation.9 | async-start | bytes 8388608
  171.9 7.8 %slice-start.1 = ((s8[6291456]{0:T(1024)(128)(4,1)}), s8[2097152]{0:T(1024)(128)(4,1)S(1)}, s32[]{:S(2)}) async-start(s8[6291456]{0:T(1024)(128)(4,1)} %bitcast.113), calls=%async_computation.10 | async-start | bytes 4194304
  171.9 7.8 %copy-start.19 = (pred[4,768]{1,0:T(4,128)(4,1)S(1)}, pred[4,768]{1,0:T(4,128)(4,1)}, u32[]{:S(2)}) copy-start(pred[4,768]{1,0:T(4,128)(4,1)} %fusion.54) | copy-start | bytes 9220
  184.3 55.7 %copy-start.10 = (bf16[16,3584]{1,0:T(8,128)(2,1)S(1)}, bf16[16,3584]{1,0:T(8,128)(2,1)}, u32[]{:S(2)}) copy-start(bf16[16,3584]{1,0:T(8,128)(2,1)} %get-tuple-element.255) | copy-start | bytes 344068
  184.3 172.4 %all-reduce.7.cloned.1.call-start = ((), (), s32[]{:S(2)}) async-start(), calls=%async_computation.5 | async-start | bytes 917504 | tf_op jit(solution)/shard_map/psum | solution.py:169
  211.7 23.1 %copy-start.12 = (f32[64,4,16]{2,1,0:T(4,128)}, f32[64,4,16]{2,1,0:T(4,128)S(1)}, u32[]{:S(2)}) copy-start(f32[64,4,16]{2,1,0:T(4,128)S(1)} %all-gather.1) | copy-start | bytes 49156
  274.0 82.7 %copy-start.4 = (bf16[16,3584]{1,0:T(8,128)(2,1)S(1)}, bf16[16,3584]{1,0:T(8,128)(2,1)}, u32[]{:S(2)}) copy-start(bf16[16,3584]{1,0:T(8,128)(2,1)} %copy-done.3) | copy-start | bytes 344068
  274.1 82.7 %copy-start.8 = (bf16[16,3584]{1,0:T(8,128)(2,1)S(1)}, bf16[16,3584]{1,0:T(8,128)(2,1)}, u32[]{:S(2)}) copy-start(bf16[16,3584]{1,0:T(8,128)(2,1)} %param.20) | copy-start | bytes 344068
  275.4 156.4 %all-reduce.11.cloned.1.call-start = ((), (), s32[]{:S(2)}) async-start(), calls=%async_computation.8 | async-start | bytes 1835008 | tf_op jit(solution)/shard_map/psum | solution.py:176
  356.7 12.9 %copy-start.5 = (bf16[896,896]{1,0:T(8,128)(2,1)S(1)}, bf16[896,896]{1,0:T(8,128)(2,1)}, u32[]{:S(2)}) copy-start(bf16[896,896]{1,0:T(8,128)(2,1)} %param.30) | copy-start | bytes 4816900
  358.1 12.9 %copy-start.1 = (bf16[16,7168]{1,0:T(8,128)(2,1)}, bf16[16,7168]{1,0:T(8,128)(2,1)S(1)}, u32[]{:S(2)}) copy-start(bf16[16,7168]{1,0:T(8,128)(2,1)S(1)} %get-tuple-element.249) | copy-start | bytes 688132
  358.1 12.8 %copy-start.6 = (bf16[896,896]{1,0:T(8,128)(2,1)S(1)}, bf16[896,896]{1,0:T(8,128)(2,1)}, u32[]{:S(2)}) copy-start(bf16[896,896]{1,0:T(8,128)(2,1)} %param.31) | copy-start | bytes 4816900
  372.2 148.9 %all-reduce.9.cloned.1.call-start = ((), (), s32[]{:S(2)}) async-start(), calls=%async_computation.7 | async-start | bytes 917504
  437.9 10.5 %all-to-all-start.1 = ((bf16[16,8,896]{2,0,1:T(8,128)(2,1)}), bf16[16,8,896]{2,0,1:T(8,128)(2,1)S(1)}, u32[]{:S(2)}, u32[]{:S(2)}) async-start(bf16[16,8,896]{2,0,1:T(8,128)(2,1)} %bitcast.123), calls=%async_computation.2 | async-start | bytes 458752 | tf_op jit(solution)/shard_map/all_to_all | solution.py:173
  (8 other events, 27.2 us)
Sparse Core Ops, SparseCore 0:
  109.4 29.5 reduce-scatter.1
  184.4 48.8 all-gather.5
  275.5 81.1 all-reduce.6
  372.3 59.4 all-reduce.10
  437.3 83.7 all-reduce.8
where the time goes:
time: 532 us; the launch traced here: 529 us
  waiting for transfers between devices  195 us (37%)
  blocking collectives  179 us (34%)
  local copies, waits for them, and re-layouts  66.7 us (13%)
  other arithmetic  40.1 us (8%)
  matrix products  26 us (5%)
  between operations  14.2 us (3%)
  starting transfers between devices  7.46 us (1%)
    psum x1, waiting for transfers between devices, body(): mixed_sum = lax.psum(projected_out, 'seq')  81.3 us
    psum x1, blocking collectives, body(): everywhere = lax.psum(looked, ('seq', 'req'))  74.1 us
    unnamed x6, waiting for transfers between devices  72.8 us
    all_gather x2, blocking collectives, merged_2(): everything = jax.tree.map(lambda part: lax.all_gather(part, axis), array)  44.8 us
    psum x1, waiting for transfers between devices, body(): lax.psum((jnp.dot(second_spread_state, gate_weight, preferred_element_typ...  34.2 us
    all_gather x1, blocking collectives, body(): lax.all_gather(qkv_part.astype(jnp.bfloat16), 'seq', axis=1, tiled=True)  24.2 us
    psum x1, blocking collectives, body(): lax.psum((jnp.dot(second_spread_state, gate_weight, preferred_element_typ...  24.2 us
    dynamic_slice x15, local copies, waits for them, and re-layouts, hop(): return combine(so_far, jax.tree.map(lambda part: part[k], everything))  14.7 us
  transfers between devices with their start and end apart: 7, of which 5 were waited for; matrix products, arithmetic and copies ran while one was open for 10% of the time, Pallas kernels for 0%

commit v1 on v0

--- a/solution.py
+++ b/solution.py
@@ -88,7 +88,7 @@
         jnp.float32
     )
     looked = jnp.where(present[:, None], looked, 0.0)
-    everywhere = lax.psum(looked, ("seq", "req"))
+    everywhere = lax.psum(lax.psum(looked, "req"), "seq")
     embedded = lax.dynamic_slice_in_dim(everywhere, req_index * group_rows, group_rows, 0)
     joined = jnp.concatenate([hidden, embedded.astype(jnp.bfloat16)], axis=1)
     normed = rms_norm(joined, attention_norm_gain)

time: 532 us -> 609 us (1.14)
  waiting for transfers between devices: 195 us -> 264 us
  blocking collectives: 179 us -> 192 us
    psum x0 -> x1, waiting for transfers between devices: none -> 64.2 us  [body(): everywhere = lax.psum(lax.psum(looked, 'req'), 'seq')]
    psum x1, blocking collectives: 74.1 us -> 89.7 us  [body(): everywhere = lax.psum(lax.psum(looked, 'req'), 'seq')]
    unnamed x6 -> x7, waiting for transfers between devices: 72.8 us -> 72.8 us
  transfers between devices with their start and end apart: 7 -> 8, of which waited for: 5 -> 6; matrix products, arithmetic and copies ran while one was open for 10% -> 8% of each run, Pallas kernels for 0% -> 0%
where the time goes in v1:
time: 609 us; the launch traced here: 606 us
  waiting for transfers between devices  264 us (43%)
  blocking collectives  192 us (32%)
  local copies, waits for them, and re-layouts  64.9 us (11%)
  other arithmetic  36.2 us (6%)
  matrix products  26.1 us (4%)
  between operations  14.5 us (2%)
  starting transfers between devices  7.31 us (1%)
    psum x1, blocking collectives, body(): everywhere = lax.psum(lax.psum(looked, 'req'), 'seq')  89.7 us
    psum x1, waiting for transfers between devices, body(): mixed_sum = lax.psum(projected_out, 'seq')  81.5 us
    unnamed x7, waiting for transfers between devices  72.8 us
    psum x1, waiting for transfers between devices, body(): everywhere = lax.psum(lax.psum(looked, 'req'), 'seq')  64.2 us
    all_gather x2, blocking collectives, merged_2(): everything = jax.tree.map(lambda part: lax.all_gather(part, axis), array)  44.8 us
    psum x1, waiting for transfers between devices, body(): lax.psum((jnp.dot(second_spread_state, gate_weight, preferred_element_typ...  34.2 us
    psum x1, blocking collectives, body(): lax.psum((jnp.dot(second_spread_state, gate_weight, preferred_element_typ...  24.2 us
    all_gather x1, blocking collectives, body(): lax.all_gather(qkv_part.astype(jnp.bfloat16), 'seq', axis=1, tiled=True)  22.2 us
  transfers between devices with their start and end apart: 8, of which 6 were waited for; matrix products, arithmetic and copies ran while one was open for 8% of the time, Pallas kernels for 0%

profile of v1, /device:TPU:0, one launch (start us, length us, event | category | flops | bytes accessed | tf_op | source)
XLA Modules:
  0.0 606.2 jit_solution(9105816548370793050)
XLA Ops:
  7.4 4.9 gather_fusion
  12.2 2.8 convert_select_fusion
  18.3 64.2 %all-reduce.8.cloned.1.call-done = f32[128,3584]{1,0:T(8,128)} async-done(((f32[128,3584]{1,0:T(8,128)}), f32[128,3584]{1,0:T(8,128)}) %all-reduce.8.cloned.1.call-update) | async-done | bytes 1835024 | tf_op jit(solution)/shard_map/psum | solution.py:91
  82.5 89.7 %all-reduce.15 = bf16[128,3584]{1,0:T(8,128)(2,1)} all-reduce(f32[128,3584]{1,0:T(8,128)} %all-reduce.8.cloned.1.call-done), channel_id=1, replica_groups=mesh['seq'=16,'req'=8] {'seq'}, use_global_device_ids=true, to_apply=%region_1.2 | all-reduce | flops 458752 | bytes 2752512 | tf_op jit(solution)/shard_map/psum | solution.py:91
  175.8 3.7 all-to-all-start
  180.9 5.8 all-to-all-done
  186.7 2.6 fusion.67
  190.1 13.2 %reshape.185 = bf16[768,16,224]{2,1,0:T(8,128)(2,1)} reshape(bf16[6,1,128,3584]{3,2,1,0:T(8,128)(2,1)} %param.24) | data formatting | bytes 11010048 | tf_op jit(solution)/shard_map/reshape | solution.py:113
  203.3 13.1 %reshape.186 = bf16[768,16,224]{2,1,0:T(8,128)(2,1)} reshape(bf16[6,1,128,3584]{3,2,1,0:T(8,128)(2,1)} %param.25) | data formatting | bytes 11010048 | tf_op jit(solution)/shard_map/reshape | solution.py:114
  218.7 22.2 %all-gather.3 = bf16[16,672,16]{1,2,0:T(8,128)(2,1)S(1)} all-gather(bf16[1,672,16]{1,2,0:T(8,128)(2,1)S(1)} %convert_bitcast_fusion), channel_id=1, replica_groups=mesh['seq'=16,'req'=8] {'seq'}, dimensions={0}, use_global_device_ids=true | all-gather | bytes 365568 | tf_op jit(solution)/shard_map/all_gather | solution.py:103
  248.8 6.8 %select_reduce_fusion = (f32[4,4,16]{1,0,2:T(4,128)S(1)}, f32[4,4,16,768]{3,1,0,2:T(4,128)S(1)}) fusion(pred[4,768]{1,0:T(4,128)(4,1)} %fusion.54, bf16[768,16,224,1]{2,1,0,3:T(8,128)(2,1)} %bitcast.116, bf16[4,4,16,112]{3,1,0,2:T(4,128)(2,1)S(1)} %get-tuple-element.268, bf16[4,4,16,112]{3,1,0,2:T(4,128)(2,1)S(1)} %get-tuple-element.269), kind=kOutput, calls=%fused_computation.25 | convolution fusion | flops 88899328 | bytes 6410240 | tf_op jit(solution)/shard_map/rthd,khd->rthk/dot_general | solution.py:129
  256.5 4.6 fusion.16
  262.4 2.3 fusion.21
  265.5 22.9 %all-gather.1 = f32[64,4,16]{2,1,0:T(4,128)S(1)} all-gather(f32[4,4,16]{2,1,0:T(4,128)S(1)} %copy.119), channel_id=3, replica_groups=mesh['seq'=16,'req'=8] {'seq'}, dimensions={0}, use_global_device_ids=true | all-gather | bytes 17408 | tf_op jit(solution)/shard_map/all_gather | solution.py:15
  288.4 21.9 %all-gather = f32[64,4,16]{2,1,0:T(4,128)S(1)} all-gather(f32[4,4,16]{2,1,0:T(4,128)} %copy.118), channel_id=2, replica_groups=mesh['seq'=16,'req'=8] {'seq'}, dimensions={0}, use_global_device_ids=true | all-gather | bytes 17408 | tf_op jit(solution)/shard_map/all_gather | solution.py:15
  318.9 29.8 %while.19 = (s32[]{:T(128)}, f32[4,4,16]{2,1,0:T(4,128)S(1)}, f32[4,4,16]{2,1,0:T(4,128)S(1)}, f32[4,4,16,224]{3,2,1,0:T(8,128)S(1)}, f32[16,4,4,16]{3,2,1,0:T(4...) while((s32[]{:T(128)}, f32[4,4,16]{2,1,0:T(4,128)S(1)}, ...), condition=%wide.region_9.10_spmd, body=%wide.region_8.9_spmd.sunk | while | flops 173573 | bytes 1157271 | solution.py:21
  352.1 81.5 %all-reduce.10.cloned.1.call-done = f32[16,7168]{1,0:T(8,128)} async-done(((f32[16,7168]{1,0:T(8,128)}), f32[16,7168]{1,0:T(8,128)}) %all-reduce.10.cloned.1.call-update) | async-done | bytes 458768 | tf_op jit(solution)/shard_map/psum | solution.py:169
  435.1 11.4 %all_to_all.54 = bf16[16,8,896]{2,0,1:T(8,128)(2,1)S(1)} all-to-all(bf16[16,8,896]{2,0,1:T(8,128)(2,1)S(1)} %bitcast.125), channel_id=1, replica_groups=mesh['seq'=16,'req'=8] {'req'}, dimensions={1} | all-to-all | bytes 458752 | tf_op jit(solution)/shard_map/all_to_all | solution.py:174
  450.3 24.2 %psum.46 = bf16[128,128]{1,0:T(8,128)(2,1)S(1)} all-reduce(f32[128,128]{1,0:T(8,128)S(1)} %fusion.70), channel_id=1, replica_groups=mesh['seq'=16,'req'=8] {'req'}, use_global_device_ids=true, to_apply=%region_15.16 | all-reduce | flops 16384 | bytes 98304 | tf_op jit(solution)/shard_map/psum | solution.py:176
  474.4 34.2 %all-reduce.14.cloned.1.call-done = (f32[128,896]{1,0:T(8,128)}, f32[128,896]{1,0:T(8,128)}) async-done(((f32[128,896]{1,0:T(8,128)}, f32[128,896]{1,0:T(8,128)}), (f32[128,896]{1,0:T(8,128)}, f32[128,896]{1,0:T(8,128)})) %all-reduce.14.cloned.1.call-update) | async-done | bytes 917520 | tf_op jit(solution)/shard_map/psum | solution.py:176
  510.8 3.2 fusion.19
  514.8 3.4 all-to-all-start.1
  519.4 5.9 all-to-all-done.1
  525.3 72.7 %all-reduce.12.cloned.1.call-done = f32[128,896]{1,0:T(8,128)} async-done(((f32[128,896]{1,0:T(8,128)}), f32[128,896]{1,0:T(8,128)}) %all-reduce.12.cloned.1.call-update) | async-done | bytes 458768
  (188 shorter events, 74.2 us)
Async XLA Ops:
  6.5 344.1 %copy-start = (bf16[224,7168]{1,0:T(8,128)(2,1)S(1)}, bf16[224,7168]{1,0:T(8,128)(2,1)}, u32[]{:S(2)}) copy-start(bf16[224,7168]{1,0:T(8,128)(2,1)} %param.28) | copy-start | bytes 9633796
  6.5 76.0 %all-reduce.8.cloned.1.call-start = ((), (), s32[]{:S(2)}) async-start(), calls=%async_computation.4 | async-start | bytes 3670016 | tf_op jit(solution)/shard_map/psum | solution.py:91
  173.2 16.1 %copy-start.3 = (bf16[16,3584]{1,0:T(8,128)(2,1)}, bf16[16,3584]{1,0:T(8,128)(2,1)S(1)}, u32[]{:S(2)}) copy-start(bf16[16,3584]{1,0:T(8,128)(2,1)S(1)} %dynamic-slice_convert_fusion) | copy-start | bytes 344068
  175.8 10.9 %all-to-all-start = ((bf16[16,8,896]{2,0,1:T(8,128)(2,1)}), bf16[16,8,896]{2,0,1:T(8,128)(2,1)S(1)}, u32[]{:S(2)}, u32[]{:S(2)}) async-start(bf16[16,8,896]{2,0,1:T(8,128)(2,1)} %copy.113), calls=%async_computation | async-start | bytes 458752 | tf_op jit(solution)/shard_map/all_to_all | solution.py:95
  179.5 38.4 %reduce-scatter.2.cloned.1.call-start = ((), (), s32[]{:S(2)}) async-start(), calls=%async_computation.5 | async-start | bytes 442368 | tf_op jit(solution)/shard_map/reduce_scatter | solution.py:97
  189.3 128.5 %all-gather.6.cloned.1.call-start = ((), (), s32[]{:S(2)}) async-start(), calls=%async_computation.7 | async-start | bytes 4456448 | tf_op jit(solution)/shard_map/all_gather | solution.py:15
  203.3 13.2 %copy-start.21 = (f32[4,4]{1,0:T(4,128)S(1)}, f32[4,4]{1,0:T(4,128)}, u32[]{:S(2)}) copy-start(f32[4,4]{1,0:T(4,128)} %add_convert_fusion.2) | copy-start | bytes 196
  203.3 14.0 %copy-start.16 = (s32[768]{0:T(1024)S(1)}, s32[768]{0:T(1024)}, u32[]{:S(2)}) copy-start(s32[768]{0:T(1024)} %iota_bitcast_fusion) | copy-start | bytes 9220
  203.3 14.0 %copy-start.17 = (pred[1,4,6,128]{3,2,1,0:T(8,128)(4,1)S(1)}, pred[1,4,6,128]{3,2,1,0:T(8,128)(4,1)}, u32[]{:S(2)}) copy-start(pred[1,4,6,128]{3,2,1,0:T(8,128)(4,1)} %broadcast_bitcast_fusion.1) | copy-start | bytes 9220
  203.3 14.0 %copy-start.24 = (s32[4]{0:T(128)S(1)}, s32[4]{0:T(128)}, u32[]{:S(2)}) copy-start(s32[4]{0:T(128)} %param.26) | copy-start | bytes 52
  247.4 9.1 %slice-start = ((s8[6291456]{0:T(1024)(128)(4,1)}), s8[4194304]{0:T(1024)(128)(4,1)S(1)}, s32[]{:S(2)}) async-start(s8[6291456]{0:T(1024)(128)(4,1)} %bitcast.113), calls=%async_computation.10 | async-start | bytes 8388608
  248.7 7.8 %slice-start.1 = ((s8[6291456]{0:T(1024)(128)(4,1)}), s8[2097152]{0:T(1024)(128)(4,1)S(1)}, s32[]{:S(2)}) async-start(s8[6291456]{0:T(1024)(128)(4,1)} %bitcast.113), calls=%async_computation.11 | async-start | bytes 4194304
  248.7 7.8 %copy-start.20 = (pred[4,768]{1,0:T(4,128)(4,1)S(1)}, pred[4,768]{1,0:T(4,128)(4,1)}, u32[]{:S(2)}) copy-start(pred[4,768]{1,0:T(4,128)(4,1)} %fusion.54) | copy-start | bytes 9220
  261.1 55.5 %copy-start.10 = (bf16[16,3584]{1,0:T(8,128)(2,1)S(1)}, bf16[16,3584]{1,0:T(8,128)(2,1)}, u32[]{:S(2)}) copy-start(bf16[16,3584]{1,0:T(8,128)(2,1)} %get-tuple-element.255) | copy-start | bytes 344068
  261.1 172.4 %all-reduce.10.cloned.1.call-start = ((), (), s32[]{:S(2)}) async-start(), calls=%async_computation.6 | async-start | bytes 917504 | tf_op jit(solution)/shard_map/psum | solution.py:169
  288.4 23.1 %copy-start.12 = (f32[64,4,16]{2,1,0:T(4,128)}, f32[64,4,16]{2,1,0:T(4,128)S(1)}, u32[]{:S(2)}) copy-start(f32[64,4,16]{2,1,0:T(4,128)S(1)} %all-gather.1) | copy-start | bytes 49156
  350.7 82.9 %copy-start.4 = (bf16[16,3584]{1,0:T(8,128)(2,1)S(1)}, bf16[16,3584]{1,0:T(8,128)(2,1)}, u32[]{:S(2)}) copy-start(bf16[16,3584]{1,0:T(8,128)(2,1)} %copy-done.3) | copy-start | bytes 344068
  350.7 82.9 %copy-start.8 = (bf16[16,3584]{1,0:T(8,128)(2,1)S(1)}, bf16[16,3584]{1,0:T(8,128)(2,1)}, u32[]{:S(2)}) copy-start(bf16[16,3584]{1,0:T(8,128)(2,1)} %param.20) | copy-start | bytes 344068
  352.0 156.6 %all-reduce.14.cloned.1.call-start = ((), (), s32[]{:S(2)}) async-start(), calls=%async_computation.9 | async-start | bytes 1835008 | tf_op jit(solution)/shard_map/psum | solution.py:176
  433.6 12.9 %copy-start.5 = (bf16[896,896]{1,0:T(8,128)(2,1)S(1)}, bf16[896,896]{1,0:T(8,128)(2,1)}, u32[]{:S(2)}) copy-start(bf16[896,896]{1,0:T(8,128)(2,1)} %param.30) | copy-start | bytes 4816900
  434.9 12.9 %copy-start.1 = (bf16[16,7168]{1,0:T(8,128)(2,1)}, bf16[16,7168]{1,0:T(8,128)(2,1)S(1)}, u32[]{:S(2)}) copy-start(bf16[16,7168]{1,0:T(8,128)(2,1)S(1)} %get-tuple-element.249) | copy-start | bytes 688132
  434.9 12.8 %copy-start.6 = (bf16[896,896]{1,0:T(8,128)(2,1)S(1)}, bf16[896,896]{1,0:T(8,128)(2,1)}, u32[]{:S(2)}) copy-start(bf16[896,896]{1,0:T(8,128)(2,1)} %param.31) | copy-start | bytes 4816900
  449.1 148.9 %all-reduce.12.cloned.1.call-start = ((), (), s32[]{:S(2)}) async-start(), calls=%async_computation.8 | async-start | bytes 917504
  514.8 10.5 %all-to-all-start.1 = ((bf16[16,8,896]{2,0,1:T(8,128)(2,1)}), bf16[16,8,896]{2,0,1:T(8,128)(2,1)S(1)}, u32[]{:S(2)}, u32[]{:S(2)}) async-start(bf16[16,8,896]{2,0,1:T(8,128)(2,1)} %bitcast.123), calls=%async_computation.2 | async-start | bytes 458752 | tf_op jit(solution)/shard_map/all_to_all | solution.py:173
  (12 other events, 39.5 us)
Sparse Core Ops, SparseCore 0:
  15.2 67.3 all-reduce.7
  189.4 26.3 reduce-scatter.1
  261.3 48.9 all-gather.5
  352.1 81.3 all-reduce.9
  449.2 59.4 all-reduce.13
  514.2 83.7 all-reduce.11
